TPU v7x, 128 devices: a whole 4x4x4 slice. The times are simulated.
128 devices in a mesh: val: 4 (over x_hi, core), cond: 8 (over z, x_lo), grid: 4 (over y).
Axes of the slice: x: 4 (x_hi: 2, x_lo: 2; x = x_hi * 2 + x_lo), y: 4, z: 4, core: 2. Of those that a mesh axis runs over, the one named last changes fastest.
Arguments:
- valence_orbitals: bfloat16 [16, 96, 9216], P('val', 'grid'), may hold values from -6 to 6
- conduction_orbitals: bfloat16 [32, 96, 9216], P('cond', 'grid'), may hold values from -6 to 6
- valence_energy: float32 [16], replicated, may hold values from -12 to -1
- conduction_energy: float32 [32], replicated, may hold values from 0.5 to 10
- grid_index: int32 [6144], replicated, may hold values from 0 to 884735, as said below
Outputs:
- response: float32 [2, 6144, 6144], P(None, ('val', 'grid'), 'cond')
Inputs may be any that keep to these rules, and one draw needn't show every extreme that they name: `grid_index`: distinct flat points of the 96 x 96 x 96 frequency grid.
All inputs are finite; a program needn't handle non-finite values.
Results may differ from a plain program's by a relative error of at most 0.0098.
Values may be sent and summed in bfloat16 or wider, within the bound.
No kernel may reach another device: no remote copies, remote signals or barrier semaphores. Data moves between devices by JAX's collectives and lax.ppermute only.
A program may use at most 128 MiB of HBM per device.

v0:
```python
import math
import jax
import jax.numpy as jnp
from jax import lax
from jax.sharding import PartitionSpec as P

NGRID = 96
NG = 6144
freq_squared = 4.0


def line_tables(points):
    indices = jnp.arange(points, dtype=jnp.int32)
    phases = indices[:, None] * indices[None, :] % points
    angles = phases.astype(jnp.float32) * (2.0 * math.pi / points)
    return (jnp.cos(angles).astype(jnp.bfloat16), (-jnp.sin(angles)).astype(jnp.bfloat16))


def plane_pass(products):
    line_cos, line_sin = line_tables(NGRID)
    z_table = jnp.concatenate([line_cos, line_sin], axis=1)
    row_total = products.shape[0]
    z_part = jnp.dot(
        products.reshape(row_total * NGRID, NGRID), z_table, preferred_element_type=jnp.float32
    )
    z_part = z_part.astype(jnp.bfloat16).reshape(row_total, NGRID, 2 * NGRID)
    first = jnp.einsum("ryk,yp->rpk", z_part, line_cos, preferred_element_type=jnp.float32)
    second = jnp.einsum("ryk,yp->rpk", z_part, line_sin, preferred_element_type=jnp.float32)
    plane_real = first[..., :NGRID] - second[..., NGRID:]
    plane_imag = second[..., :NGRID] + first[..., NGRID:]
    return jnp.concatenate([plane_real, plane_imag], axis=-1).astype(jnp.bfloat16)


def band_spectra(orbital, conduction_part):
    products = (orbital.astype(jnp.float32)[None] * conduction_part.astype(jnp.float32)).astype(
        jnp.bfloat16
    )
    band_total = conduction_part.shape[0]
    depth = conduction_part.shape[1]
    spectra = plane_pass(products.reshape(band_total * depth, NGRID, NGRID))
    return spectra.reshape(band_total, depth, NGRID, 2 * NGRID)


def line_pick(pieces, grid_index, row_offset):
    line_cos, line_sin = line_tables(NGRID)
    pair_total = pieces.shape[0]
    local_rows = pieces.shape[2]
    split = pieces.reshape(pair_total, NGRID, local_rows, 2, NGRID)
    table_rows = jnp.transpose(split, (2, 4, 1, 0, 3)).reshape(
        local_rows * NGRID, NGRID, pair_total * 2
    )
    plane_size = NGRID * NGRID
    vector_total = grid_index.shape[0]
    line_number = grid_index // plane_size
    remainder = grid_index % plane_size
    local_row = remainder // NGRID - row_offset
    column = remainder % NGRID
    inside = (local_row >= 0) & (local_row < local_rows)
    row_index = jnp.clip(local_row, 0, local_rows - 1) * NGRID + column
    block = math.gcd(vector_total, 512)
    count = vector_total // block
    scale = NGRID ** (-1.5)
    factor = jnp.where(inside, scale, 0.0).astype(jnp.float32)
    frequencies = jnp.arange(NGRID, dtype=jnp.int32)

    def one_block(item):
        lines, picks, keep = item
        picked = jnp.take(table_rows, picks, axis=0).reshape(block, NGRID, pair_total, 2)
        onehot = (lines[:, None] == frequencies[None, :]).astype(jnp.bfloat16)
        cos_pick = jnp.dot(onehot, line_cos.T, preferred_element_type=jnp.float32).astype(
            jnp.bfloat16
        )
        sin_pick = jnp.dot(onehot, line_sin.T, preferred_element_type=jnp.float32).astype(
            jnp.bfloat16
        )
        real_part = picked[..., 0]
        imag_part = picked[..., 1]
        real_out = jnp.einsum(
            "jx,jxp->jp", cos_pick, real_part, preferred_element_type=jnp.float32
        ) - jnp.einsum("jx,jxp->jp", sin_pick, imag_part, preferred_element_type=jnp.float32)
        imag_out = jnp.einsum(
            "jx,jxp->jp", sin_pick, real_part, preferred_element_type=jnp.float32
        ) + jnp.einsum("jx,jxp->jp", cos_pick, imag_part, preferred_element_type=jnp.float32)
        return jnp.stack([real_out * keep[:, None], imag_out * keep[:, None]])

    blocks = lax.map(
        one_block,
        (
            line_number.reshape(count, block),
            row_index.reshape(count, block),
            factor.reshape(count, block),
        ),
    )
    result = jnp.transpose(blocks, (1, 3, 0, 2)).reshape(2, pair_total, vector_total)
    return result.astype(jnp.bfloat16)


def local(valence_orbitals, conduction_orbitals, valence_energy, conduction_energy, grid_index):
    valence_groups = lax.axis_size("val")
    conduction_groups = lax.axis_size("cond")
    grid_groups = lax.axis_size("grid")
    valence_local = valence_orbitals.shape[0]
    conduction_local = conduction_orbitals.shape[0]
    pair_count = valence_local * conduction_local
    slab_depth = valence_orbitals.shape[1]

    def one_valence(orbital):
        return band_spectra(orbital, conduction_orbitals)

    spectra = lax.map(one_valence, valence_orbitals)
    spectra = spectra.reshape(pair_count, slab_depth, NGRID, 2 * NGRID)
    row_offset = lax.axis_index("grid") * (NGRID // grid_groups)
    partial_values = line_pick(
        lax.all_to_all(spectra, "grid", split_axis=2, concat_axis=1, tiled=True),
        grid_index,
        row_offset,
    )
    pair_values = lax.psum(partial_values.astype(jnp.float32).astype(jnp.bfloat16), "grid")
    delta = valence_energy[:, None] - conduction_energy[None, :]
    all_pairs = valence_energy.shape[0] * conduction_energy.shape[0]
    weights = 4.0 * delta / (delta * delta + freq_squared) / math.sqrt(all_pairs)
    weights = weights.reshape(valence_groups, valence_local, conduction_groups, conduction_local)
    weights = jnp.transpose(weights, (0, 2, 1, 3)).reshape(all_pairs)
    row_width = NG // (valence_groups * grid_groups)
    split_view = pair_values.reshape(2, pair_count, valence_groups, grid_groups, row_width)
    grid_rows = lax.dynamic_index_in_dim(split_view, lax.axis_index("grid"), 3, keepdims=False)
    everything = lax.all_gather(
        grid_rows.reshape(2, pair_count, valence_groups * row_width),
        ("val", "cond"),
        axis=1,
        tiled=True,
    )
    row_values = lax.dynamic_slice_in_dim(
        everything, lax.axis_index("val") * row_width, row_width, 2
    )
    scaled_rows = (row_values.astype(jnp.float32) * weights[None, :, None]).astype(jnp.bfloat16)
    by_column = lax.all_to_all(pair_values, "cond", split_axis=2, concat_axis=1, tiled=True)
    contract = (((0,), (0,)), ((), ()))
    piece = lax.all_gather(by_column, "val", axis=1, tiled=True)
    real_sum = lax.dot_general(
        scaled_rows[0], piece[0], contract, preferred_element_type=jnp.float32
    )
    real_sum = real_sum + lax.dot_general(
        scaled_rows[1], piece[1], contract, preferred_element_type=jnp.float32
    )
    imag_sum = lax.dot_general(
        scaled_rows[1], piece[0], contract, preferred_element_type=jnp.float32
    )
    imag_sum = imag_sum - lax.dot_general(
        scaled_rows[0], piece[1], contract, preferred_element_type=jnp.float32
    )
    return jnp.stack([real_sum, imag_sum])


def solution(mesh):
    return jax.shard_map(
        local,
        mesh=mesh,
        in_specs=(P("val", "grid", None), P("cond", "grid", None), P(), P(), P()),
        out_specs=P(None, ("val", "grid"), "cond"),
        check_vma=False,
    )
```

profile of v0, /device:TPU:1, one launch (start us, length us, event | category | flops | bytes accessed | tf_op | source)
XLA Modules:
  0.0 897.4 jit_solution(11764834540841196857)
XLA Ops:
  6.5 128.8 %while.23 = (s32[]{:T(128)}, bf16[4,4,24,96,192]{4,2,1,0,3:T(8,128)(2,1)}, bf16[4,24,9216]{2,1,0:T(8,128)(2,1)}, bf16[4,24,9216]{2,1,0:T(8,128)(2,1)}, s32[]{:T(128)}) while((s32[]{:T(128)}, bf16[4,4,24,96,192]{4,2,1,0,3:T(8,128)(2,1)}, bf16[4,24,9216]{2,1,0:T(8,128)(2,1)}, bf16[4,24,9216]{2,1,0:T(8,128)(2,1)}, s32[]{:T(128)}) %tuple.68), condition=%wide.region_1.2_spmd, body=%wide.region_0.1_spmd.sunk | while | flops 1034855424 | bytes 90169952 | solution.py:110
  9.4 3.3 convert_element_type.200
  13.0 2.8 convolution_convert_fusion.4
  15.7 3.9 copy.96
  19.7 4.1 convolution_bitcast_fusion.4
  25.3 4.0 fusion.84
  29.3 4.4 pad_maximum_fusion.3
  33.8 4.9 copy_dynamic-update-slice_fusion.2
  41.6 3.3 convert_element_type.200
  47.9 3.9 copy.96
  51.8 4.1 convolution_bitcast_fusion.4
  57.5 4.0 fusion.84
  61.5 4.4 pad_maximum_fusion.3
  65.9 4.9 copy_dynamic-update-slice_fusion.2
  73.7 3.3 convert_element_type.200
  80.0 3.9 copy.96
  84.0 4.1 convolution_bitcast_fusion.4
  89.6 4.0 fusion.84
  93.6 4.4 pad_maximum_fusion.3
  98.0 5.1 copy_dynamic-update-slice_fusion.2
  106.0 3.3 convert_element_type.200
  112.3 3.9 copy.96
  116.2 4.1 convolution_bitcast_fusion.4
  121.9 4.0 fusion.84
  125.9 4.4 pad_maximum_fusion.3
  130.3 5.0 copy_dynamic-update-slice_fusion.2
  135.3 7.7 all-to-all-start
  144.5 204.8 %all-to-all-done = bf16[16,24,96,192]{3,1,0,2:T(8,128)(2,1)} async-done(((bf16[16,24,96,192]{3,1,0,2:T(8,128)(2,1)}), bf16[16,24,96,192]{3,1,0,2:T(8,128)(2,1)}, u32[]{:S(2)}, u32[]{:S(2)}) %all-to-all-start) | async-done | bytes 14155808 | tf_op jit(solution)/shard_map/all_to_all | solution.py:114
  349.3 35.3 %copy.48 = bf16[16,4,24,24,192]{4,3,2,1,0:T(8,128)(2,1)} copy(bf16[16,4,24,24,192]{4,2,0,3,1:T(8,128)(2,1)} %bitcast.10) | data formatting | bytes 28311552 | tf_op jit(solution)/shard_map/all_to_all | solution.py:114
  384.6 29.6 %reshape.152 = bf16[16,96,24,2,96]{4,3,2,1,0:T(2,128)(2,1)} reshape(bf16[16,4,24,24,192]{4,3,2,1,0:T(8,128)(2,1)} %copy.48) | data formatting | bytes 28311552 | tf_op jit(solution)/shard_map/reshape | solution.py:48
  414.2 60.5 %copy.73 = bf16[24,96,96,16,2]{2,4,3,1,0:T(2,128)(2,1)} copy(bf16[24,96,96,16,2]{1,4,0,2,3:T(2,128)(2,1)} %bitcast.126) | data formatting | bytes 28311552
  474.7 250.2 %while.24 = (s32[]{:T(128)}, bf16[12,2,512,16]{2,3,1,0:T(8,128)(2,1)S(1)}, s32[12,512]{1,0:T(8,128)}, s32[12,512]{1,0:T(8,128)S(1)}, bf16[2304,96,32]{1,2,0:T(8,128)(2,1)}, /*index=5*/f32[12,512]{1,0:T(8,128)}, s32[]{:T(128)}) while((s32[]{:T(128)}, bf16[12,2,512,16]{2,3,1,0:T(8,128)(2,1)S(1)}, s32[12,512]{1,0:T(8,128)}, ...), condition=%wide.region_3.4_spmd.clone, body=%wide.region_2.3_spmd.clone.sunk | while | flops 28887552 | bytes 29686932 | solution.py:86
  475.3 9.6 %gather_fusion = bf16[512,96,32]{1,2,0:T(8,128)(2,1)} fusion(bf16[2304,96,32]{1,2,0:T(8,128)(2,1)} %get-tuple-element.309, s32[1024]{0:T(1024)S(1)} %pad_clamp_fusion.2), kind=kCustom, calls=%fused_computation.clone.clone.1 | custom fusion | bytes 6293504 | tf_op jit(solution)/shard_map/while/body/eval_jaxpr/jit(_take)/gather | solution.py:68
  484.9 5.8 copy.98
  496.1 9.6 %gather_fusion = bf16[512,96,32]{1,2,0:T(8,128)(2,1)} fusion(bf16[2304,96,32]{1,2,0:T(8,128)(2,1)} %get-tuple-element.309, s32[1024]{0:T(1024)S(1)} %pad_clamp_fusion.2), kind=kCustom, calls=%fused_computation.clone.clone.1 | custom fusion | bytes 6293504 | tf_op jit(solution)/shard_map/while/body/eval_jaxpr/jit(_take)/gather | solution.py:68
  505.7 5.8 copy.98
  517.0 9.6 %gather_fusion = bf16[512,96,32]{1,2,0:T(8,128)(2,1)} fusion(bf16[2304,96,32]{1,2,0:T(8,128)(2,1)} %get-tuple-element.309, s32[1024]{0:T(1024)S(1)} %pad_clamp_fusion.2), kind=kCustom, calls=%fused_computation.clone.clone.1 | custom fusion | bytes 6293504 | tf_op jit(solution)/shard_map/while/body/eval_jaxpr/jit(_take)/gather | solution.py:68
  526.6 5.8 copy.98
  537.8 9.6 %gather_fusion = bf16[512,96,32]{1,2,0:T(8,128)(2,1)} fusion(bf16[2304,96,32]{1,2,0:T(8,128)(2,1)} %get-tuple-element.309, s32[1024]{0:T(1024)S(1)} %pad_clamp_fusion.2), kind=kCustom, calls=%fused_computation.clone.clone.1 | custom fusion | bytes 6293504 | tf_op jit(solution)/shard_map/while/body/eval_jaxpr/jit(_take)/gather | solution.py:68
  547.4 5.8 copy.98
  558.7 9.6 %gather_fusion = bf16[512,96,32]{1,2,0:T(8,128)(2,1)} fusion(bf16[2304,96,32]{1,2,0:T(8,128)(2,1)} %get-tuple-element.309, s32[1024]{0:T(1024)S(1)} %pad_clamp_fusion.2), kind=kCustom, calls=%fused_computation.clone.clone.1 | custom fusion | bytes 6293504 | tf_op jit(solution)/shard_map/while/body/eval_jaxpr/jit(_take)/gather | solution.py:68
  568.3 5.8 copy.98
  579.5 9.6 %gather_fusion = bf16[512,96,32]{1,2,0:T(8,128)(2,1)} fusion(bf16[2304,96,32]{1,2,0:T(8,128)(2,1)} %get-tuple-element.309, s32[1024]{0:T(1024)S(1)} %pad_clamp_fusion.2), kind=kCustom, calls=%fused_computation.clone.clone.1 | custom fusion | bytes 6293504 | tf_op jit(solution)/shard_map/while/body/eval_jaxpr/jit(_take)/gather | solution.py:68
  589.1 5.8 copy.98
  600.4 9.6 %gather_fusion = bf16[512,96,32]{1,2,0:T(8,128)(2,1)} fusion(bf16[2304,96,32]{1,2,0:T(8,128)(2,1)} %get-tuple-element.309, s32[1024]{0:T(1024)S(1)} %pad_clamp_fusion.2), kind=kCustom, calls=%fused_computation.clone.clone.1 | custom fusion | bytes 6293504 | tf_op jit(solution)/shard_map/while/body/eval_jaxpr/jit(_take)/gather | solution.py:68
  610.0 5.8 copy.98
  621.2 9.6 %gather_fusion = bf16[512,96,32]{1,2,0:T(8,128)(2,1)} fusion(bf16[2304,96,32]{1,2,0:T(8,128)(2,1)} %get-tuple-element.309, s32[1024]{0:T(1024)S(1)} %pad_clamp_fusion.2), kind=kCustom, calls=%fused_computation.clone.clone.1 | custom fusion | bytes 6293504 | tf_op jit(solution)/shard_map/while/body/eval_jaxpr/jit(_take)/gather | solution.py:68
  630.8 5.8 copy.98
  642.1 9.6 %gather_fusion = bf16[512,96,32]{1,2,0:T(8,128)(2,1)} fusion(bf16[2304,96,32]{1,2,0:T(8,128)(2,1)} %get-tuple-element.309, s32[1024]{0:T(1024)S(1)} %pad_clamp_fusion.2), kind=kCustom, calls=%fused_computation.clone.clone.1 | custom fusion | bytes 6293504 | tf_op jit(solution)/shard_map/while/body/eval_jaxpr/jit(_take)/gather | solution.py:68
  651.7 5.8 copy.98
  662.9 9.6 %gather_fusion = bf16[512,96,32]{1,2,0:T(8,128)(2,1)} fusion(bf16[2304,96,32]{1,2,0:T(8,128)(2,1)} %get-tuple-element.309, s32[1024]{0:T(1024)S(1)} %pad_clamp_fusion.2), kind=kCustom, calls=%fused_computation.clone.clone.1 | custom fusion | bytes 6293504 | tf_op jit(solution)/shard_map/while/body/eval_jaxpr/jit(_take)/gather | solution.py:68
  672.5 5.8 copy.98
  683.8 9.6 %gather_fusion = bf16[512,96,32]{1,2,0:T(8,128)(2,1)} fusion(bf16[2304,96,32]{1,2,0:T(8,128)(2,1)} %get-tuple-element.309, s32[1024]{0:T(1024)S(1)} %pad_clamp_fusion.2), kind=kCustom, calls=%fused_computation.clone.clone.1 | custom fusion | bytes 6293504 | tf_op jit(solution)/shard_map/while/body/eval_jaxpr/jit(_take)/gather | solution.py:68
  693.4 5.8 copy.98
  704.6 9.6 %gather_fusion = bf16[512,96,32]{1,2,0:T(8,128)(2,1)} fusion(bf16[2304,96,32]{1,2,0:T(8,128)(2,1)} %get-tuple-element.309, s32[1024]{0:T(1024)S(1)} %pad_clamp_fusion.2), kind=kCustom, calls=%fused_computation.clone.clone.1 | custom fusion | bytes 6293504 | tf_op jit(solution)/shard_map/while/body/eval_jaxpr/jit(_take)/gather | solution.py:68
  714.2 5.8 copy.98
  725.7 41.6 %all-reduce.2.cloned.1.call-done = bf16[2,16,6144]{2,1,0:T(8,128)(2,1)} async-done(((bf16[2,16,6144]{2,1,0:T(8,128)(2,1)}), bf16[2,16,6144]{2,1,0:T(8,128)(2,1)}) %all-reduce.2.cloned.1.call-update) | async-done | bytes 393232 | tf_op jit(solution)/shard_map/psum | solution.py:118
  770.0 6.1 copy.53
  776.1 3.3 reshape.183
  779.4 12.1 %all_to_all.33 = bf16[8,2,12288]{2,1,0:T(2,128)(2,1)} all-to-all(bf16[8,2,12288]{2,1,0:T(2,128)(2,1)S(1)} %reshape.183), channel_id=1, replica_groups=mesh['val'=4,'cond'=8,'grid'=4] {'cond'}, dimensions={0} | all-to-all | bytes 786432 | tf_op jit(solution)/shard_map/all_to_all | solution.py:137
  791.5 10.2 %reshape.184 = bf16[6144,2,16]{2,1,0:T(2,128)(2,1)S(1)} reshape(bf16[8,2,12288]{2,1,0:T(2,128)(2,1)} %all_to_all.33) | data formatting | bytes 786432
  801.7 4.8 copy.75
  806.9 51.1 %all-gather.3.cloned.1.call-done = bf16[2,512,1536]{2,1,0:T(8,128)(2,1)} async-done(((bf16[2,16,1536]{2,1,0:T(8,128)(2,1)}), bf16[2,512,1536]{2,1,0:T(8,128)(2,1)}) %all-gather.3.cloned.1.call-update) | async-done | bytes 3145744 | tf_op jit(solution)/shard_map/all_gather | solution.py:127
  859.4 25.5 %all-gather.5.cloned.1.call-done = bf16[2,512,768]{2,1,0:T(8,128)(2,1)} async-done(((bf16[2,128,768]{2,1,0:T(8,128)(2,1)}), bf16[2,512,768]{2,1,0:T(8,128)(2,1)}) %all-gather.5.cloned.1.call-update) | async-done | bytes 1572880 | tf_op jit(solution)/shard_map/all_gather | solution.py:139
  (254 shorter events, 104.0 us)
Async XLA Ops:
  19.7 4.1 copy-start
  51.8 4.1 copy-start
  84.0 4.1 copy-start
  116.2 4.1 copy-start
  135.3 7.8 copy-start.2
  135.3 213.9 %all-to-all-start = ((bf16[16,24,96,192]{3,1,0,2:T(8,128)(2,1)}), bf16[16,24,96,192]{3,1,0,2:T(8,128)(2,1)}, u32[]{:S(2)}, u32[]{:S(2)}) async-start(bf16[16,24,96,192]{3,1,0,2:T(8,128)(2,1)} %bitcast.127), calls=%async_computation | async-start | bytes 37748736 | tf_op jit(solution)/shard_map/all_to_all | solution.py:114
  143.1 624.3 %all-reduce.2.cloned.1.call-start = ((), (), s32[]{:S(2)}) async-start(), calls=%async_computation.2 | async-start | bytes 786432 | tf_op jit(solution)/shard_map/psum | solution.py:118
  474.7 0.6 copy-start.3
  491.2 4.3 copy-start.4
  495.5 0.6 copy-start.3
  512.0 4.3 copy-start.4
  516.4 0.6 copy-start.3
  532.9 4.3 copy-start.4
  537.2 0.6 copy-start.3
  553.7 4.3 copy-start.4
  558.1 0.6 copy-start.3
  574.6 4.3 copy-start.4
  578.9 0.6 copy-start.3
  595.4 4.3 copy-start.4
  599.8 0.6 copy-start.3
  616.3 4.3 copy-start.4
  620.6 0.6 copy-start.3
  637.1 4.3 copy-start.4
  641.5 0.6 copy-start.3
  658.0 4.3 copy-start.4
  662.3 0.6 copy-start.3
  678.8 4.3 copy-start.4
  683.2 0.6 copy-start.3
  699.7 4.3 copy-start.4
  704.0 0.6 copy-start.3
  720.5 4.3 copy-start.4
  725.7 132.3 %all-gather.3.cloned.1.call-start = ((), (), s32[]{:S(2)}) async-start(), calls=%async_computation.3 | async-start | bytes 3244032 | tf_op jit(solution)/shard_map/all_gather | solution.py:127
  770.0 114.9 %all-gather.5.cloned.1.call-start = ((), (), s32[]{:S(2)}) async-start(), calls=%async_computation.4 | async-start | bytes 1966080 | tf_op jit(solution)/shard_map/all_gather | solution.py:139
  791.5 15.0 %copy-start.5 = (f32[32]{0:T(128)S(1)}, f32[32]{0:T(128)}, u32[]{:S(2)}) copy-start(f32[32]{0:T(128)} %param.12) | copy-start | bytes 388
  791.5 15.1 %copy-start.6 = (f32[16]{0:T(128)S(1)}, f32[16]{0:T(128)}, u32[]{:S(2)}) copy-start(f32[16]{0:T(128)} %param.11) | copy-start | bytes 196
  884.8 3.4 copy-start.1
Sparse Core Ops, SparseCore 0:
  725.8 41.5 all-reduce.1
  770.1 87.8 all-gather.2
  859.7 25.0 all-gather.4
where the time goes:
time: 904 us; the launch traced here: 897 us
  local copies, waits for them, and re-layouts  415 us (46%)
  waiting for transfers between devices  323 us (36%)
  other arithmetic  77.3 us (9%)
  matrix products  47.5 us (5%)
  between operations  13.3 us (1%)
  blocking collectives  12.1 us (1%)
    all_to_all x1, waiting for transfers between devices, local(): lax.all_to_all(spectra, 'grid', split_axis=2, concat_axis=1, tiled=True)  205 us
    gather x24, local copies, waits for them, and re-layouts, one_block(): jnp.take(table_rows, picks, axis=0).reshape(block, NGRID, pair_total, 2)  184 us
    unnamed x11, local copies, waits for them, and re-layouts  73.9 us
    all_gather x1, waiting for transfers between devices, local(): lax.all_gather(grid_rows.reshape(2, pair_count, valence_groups * row_widt...  51.1 us
    psum x1, waiting for transfers between devices, local(): lax.psum(partial_values.astype(jnp.float32).astype(jnp.bfloat16), 'grid')  41.6 us
    all_to_all x1, local copies, waits for them, and re-layouts, local(): lax.all_to_all(spectra, 'grid', split_axis=2, concat_axis=1, tiled=True)  35.3 us
    reshape x1, local copies, waits for them, and re-layouts, line_pick(): split = pieces.reshape(pair_total, NGRID, local_rows, 2, NGRID)  29.6 us
    all_gather x1, waiting for transfers between devices, local(): piece = lax.all_gather(by_column, 'val', axis=1, tiled=True)  25.5 us
  transfers between devices with their start and end apart: 4, of which 4 were waited for; matrix products, arithmetic and copies ran while one was open for 3% of the time, Pallas kernels for 0%

commit v1 on v0

--- a/solution.py
+++ b/solution.py
@@ -124,11 +124,17 @@
     row_width = NG // (valence_groups * grid_groups)
     split_view = pair_values.reshape(2, pair_count, valence_groups, grid_groups, row_width)
     grid_rows = lax.dynamic_index_in_dim(split_view, lax.axis_index("grid"), 3, keepdims=False)
-    everything = lax.all_gather(
-        grid_rows.reshape(2, pair_count, valence_groups * row_width),
-        ("val", "cond"),
+    everything = jnp.concatenate(
+        lax.all_to_all(
+            jnp.stack(
+                [grid_rows.reshape(2, pair_count, valence_groups * row_width)]
+                * lax.axis_size(("val", "cond"))
+            ),
+            ("val", "cond"),
+            0,
+            0,
+        ),
         axis=1,
-        tiled=True,
     )
     row_values = lax.dynamic_slice_in_dim(
         everything, lax.axis_index("val") * row_width, row_width, 2

time: 904 us -> 868 us (0.960)
  waiting for transfers between devices: 323 us -> 288 us
  starting transfers between devices: 7.85 us -> 21.6 us
  blocking collectives: 12.1 us -> 0 us
    all_gather x1 -> x0, waiting for transfers between devices: 51.1 us -> none  [local(): lax.all_gather(grid_rows.reshape(2, pair_count, valence_groups * row_widt...]
    all_to_all x0 -> x2, waiting for transfers between devices: none -> 41.1 us  [the longest x1 36.2 us: local(): lax.all_to_all(jnp.stack([grid_rows.reshape(2, pair_count, valence_groups...]
    all_gather x1, waiting for transfers between devices: 25.5 us -> 0.02 us  [local(): piece = lax.all_gather(by_column, 'val', axis=1, tiled=True)]
    all_to_all x0 -> x2, starting transfers between devices: none -> 13.8 us  [the longest x1 8.76 us: local(): lax.all_to_all(jnp.stack([grid_rows.reshape(2, pair_count, valence_groups...]
    all_to_all x1 -> x0, blocking collectives: 12.1 us -> none  [local(): lax.all_to_all(pair_values, 'cond', split_axis=2, concat_axis=1, tiled=True)]
  transfers between devices with their start and end apart: 4 -> 5, of which waited for: 4 -> 4; matrix products, arithmetic and copies ran while one was open for 3% -> 2% of each run, Pallas kernels for 0% -> 0%
where the time goes in v1:
time: 868 us; the launch traced here: 861 us
  local copies, waits for them, and re-layouts  414 us (48%)
  waiting for transfers between devices  288 us (33%)
  other arithmetic  76.2 us (9%)
  matrix products  47.6 us (5%)
  starting transfers between devices  21.6 us (2%)
  between operations  13.6 us (2%)
    all_to_all x1, waiting for transfers between devices, local(): lax.all_to_all(spectra, 'grid', split_axis=2, concat_axis=1, tiled=True)  205 us
    gather x24, local copies, waits for them, and re-layouts, one_block(): jnp.take(table_rows, picks, axis=0).reshape(block, NGRID, pair_total, 2)  185 us
    unnamed x11, local copies, waits for them, and re-layouts  67.7 us
    psum x1, waiting for transfers between devices, local(): lax.psum(partial_values.astype(jnp.float32).astype(jnp.bfloat16), 'grid')  41.7 us
    all_to_all x1, waiting for transfers between devices, local(): lax.all_to_all(jnp.stack([grid_rows.reshape(2, pair_count, valence_groups...  36.2 us
    all_to_all x1, local copies, waits for them, and re-layouts, local(): lax.all_to_all(spectra, 'grid', split_axis=2, concat_axis=1, tiled=True)  35.4 us
    reshape x1, local copies, waits for them, and re-layouts, line_pick(): split = pieces.reshape(pair_total, NGRID, local_rows, 2, NGRID)  29.5 us
    dot_general x12, other arithmetic, one_block(): jnp.einsum('jx,jxp->jp', cos_pick, real_part, preferred_element_type=jnp....  24.1 us
  transfers between devices with their start and end apart: 5, of which 4 were waited for; matrix products, arithmetic and copies ran while one was open for 2% of the time, Pallas kernels for 0%

profile of v1, /device:TPU:1, one launch (start us, length us, event | category | flops | bytes accessed | tf_op | source)
XLA Modules:
  0.0 861.5 jit_solution(11609377670470530388)
XLA Ops:
  6.5 128.8 %while.23 = (s32[]{:T(128)}, bf16[4,4,24,96,192]{4,2,1,0,3:T(8,128)(2,1)}, bf16[4,24,9216]{2,1,0:T(8,128)(2,1)}, bf16[4,24,9216]{2,1,0:T(8,128)(2,1)}, s32[]{:T(128)}) while((s32[]{:T(128)}, bf16[4,4,24,96,192]{4,2,1,0,3:T(8,128)(2,1)}, bf16[4,24,9216]{2,1,0:T(8,128)(2,1)}, bf16[4,24,9216]{2,1,0:T(8,128)(2,1)}, s32[]{:T(128)}) %tuple.68), condition=%wide.region_1.2_spmd, body=%wide.region_0.1_spmd.sunk | while | flops 1034855424 | bytes 90169952 | solution.py:110
  9.4 3.3 convert_element_type.200
  15.7 4.0 copy.98
  19.7 4.1 convolution_bitcast_fusion.4
  25.3 4.0 fusion.84
  29.3 4.4 pad_maximum_fusion.3
  33.8 4.9 copy_dynamic-update-slice_fusion.2
  41.6 3.3 convert_element_type.200
  47.9 4.0 copy.98
  51.9 4.1 convolution_bitcast_fusion.4
  57.5 4.0 fusion.84
  61.5 4.4 pad_maximum_fusion.3
  66.0 5.0 copy_dynamic-update-slice_fusion.2
  73.8 3.3 convert_element_type.200
  80.1 4.0 copy.98
  84.1 4.1 convolution_bitcast_fusion.4
  89.7 4.0 fusion.84
  93.8 4.4 pad_maximum_fusion.3
  98.2 5.0 copy_dynamic-update-slice_fusion.2
  106.0 3.3 convert_element_type.200
  112.4 4.0 copy.98
  116.3 4.1 convolution_bitcast_fusion.4
  122.0 4.0 fusion.84
  126.0 4.4 pad_maximum_fusion.3
  130.4 4.9 copy_dynamic-update-slice_fusion.2
  135.3 7.7 all-to-all-start
  144.5 204.8 %all-to-all-done = bf16[16,24,96,192]{3,1,0,2:T(8,128)(2,1)} async-done(((bf16[16,24,96,192]{3,1,0,2:T(8,128)(2,1)}), bf16[16,24,96,192]{3,1,0,2:T(8,128)(2,1)}, u32[]{:S(2)}, u32[]{:S(2)}) %all-to-all-start) | async-done | bytes 14155808 | tf_op jit(solution)/shard_map/all_to_all | solution.py:114
  349.3 35.4 %copy.49 = bf16[16,4,24,24,192]{4,3,2,1,0:T(8,128)(2,1)} copy(bf16[16,4,24,24,192]{4,2,0,3,1:T(8,128)(2,1)} %bitcast.10) | data formatting | bytes 28311552 | tf_op jit(solution)/shard_map/all_to_all | solution.py:114
  384.7 29.5 %reshape.157 = bf16[16,96,24,2,96]{4,3,2,1,0:T(2,128)(2,1)} reshape(bf16[16,4,24,24,192]{4,3,2,1,0:T(8,128)(2,1)} %copy.49) | data formatting | bytes 28311552 | tf_op jit(solution)/shard_map/reshape | solution.py:48
  414.2 60.5 %copy.75 = bf16[24,96,96,16,2]{2,4,3,1,0:T(2,128)(2,1)} copy(bf16[24,96,96,16,2]{1,4,0,2,3:T(2,128)(2,1)} %bitcast.129) | data formatting | bytes 28311552
  474.7 250.3 %while.24 = (s32[]{:T(128)}, bf16[12,2,512,16]{2,3,1,0:T(8,128)(2,1)S(1)}, s32[12,512]{1,0:T(8,128)}, s32[12,512]{1,0:T(8,128)S(1)}, bf16[2304,96,32]{1,2,0:T(8,128)(2,1)}, /*index=5*/f32[12,512]{1,0:T(8,128)}, s32[]{:T(128)}) while((s32[]{:T(128)}, bf16[12,2,512,16]{2,3,1,0:T(8,128)(2,1)S(1)}, s32[12,512]{1,0:T(8,128)}, ...), condition=%wide.region_3.4_spmd.clone, body=%wide.region_2.3_spmd.clone.sunk | while | flops 28887552 | bytes 29686932 | solution.py:86
  475.3 9.6 %gather_fusion = bf16[512,96,32]{1,2,0:T(8,128)(2,1)} fusion(bf16[2304,96,32]{1,2,0:T(8,128)(2,1)} %get-tuple-element.309, s32[1024]{0:T(1024)S(1)} %pad_clamp_fusion.2), kind=kCustom, calls=%fused_computation.clone.clone.1 | custom fusion | bytes 6293504 | tf_op jit(solution)/shard_map/while/body/eval_jaxpr/jit(_take)/gather | solution.py:68
  484.9 5.8 copy.100
  496.2 9.6 %gather_fusion = bf16[512,96,32]{1,2,0:T(8,128)(2,1)} fusion(bf16[2304,96,32]{1,2,0:T(8,128)(2,1)} %get-tuple-element.309, s32[1024]{0:T(1024)S(1)} %pad_clamp_fusion.2), kind=kCustom, calls=%fused_computation.clone.clone.1 | custom fusion | bytes 6293504 | tf_op jit(solution)/shard_map/while/body/eval_jaxpr/jit(_take)/gather | solution.py:68
  505.8 5.8 copy.100
  517.1 9.6 %gather_fusion = bf16[512,96,32]{1,2,0:T(8,128)(2,1)} fusion(bf16[2304,96,32]{1,2,0:T(8,128)(2,1)} %get-tuple-element.309, s32[1024]{0:T(1024)S(1)} %pad_clamp_fusion.2), kind=kCustom, calls=%fused_computation.clone.clone.1 | custom fusion | bytes 6293504 | tf_op jit(solution)/shard_map/while/body/eval_jaxpr/jit(_take)/gather | solution.py:68
  526.7 5.8 copy.100
  537.9 9.6 %gather_fusion = bf16[512,96,32]{1,2,0:T(8,128)(2,1)} fusion(bf16[2304,96,32]{1,2,0:T(8,128)(2,1)} %get-tuple-element.309, s32[1024]{0:T(1024)S(1)} %pad_clamp_fusion.2), kind=kCustom, calls=%fused_computation.clone.clone.1 | custom fusion | bytes 6293504 | tf_op jit(solution)/shard_map/while/body/eval_jaxpr/jit(_take)/gather | solution.py:68
  547.5 5.8 copy.100
  558.8 9.6 %gather_fusion = bf16[512,96,32]{1,2,0:T(8,128)(2,1)} fusion(bf16[2304,96,32]{1,2,0:T(8,128)(2,1)} %get-tuple-element.309, s32[1024]{0:T(1024)S(1)} %pad_clamp_fusion.2), kind=kCustom, calls=%fused_computation.clone.clone.1 | custom fusion | bytes 6293504 | tf_op jit(solution)/shard_map/while/body/eval_jaxpr/jit(_take)/gather | solution.py:68
  568.4 5.8 copy.100
  579.6 9.6 %gather_fusion = bf16[512,96,32]{1,2,0:T(8,128)(2,1)} fusion(bf16[2304,96,32]{1,2,0:T(8,128)(2,1)} %get-tuple-element.309, s32[1024]{0:T(1024)S(1)} %pad_clamp_fusion.2), kind=kCustom, calls=%fused_computation.clone.clone.1 | custom fusion | bytes 6293504 | tf_op jit(solution)/shard_map/while/body/eval_jaxpr/jit(_take)/gather | solution.py:68
  589.2 5.8 copy.100
  600.5 9.6 %gather_fusion = bf16[512,96,32]{1,2,0:T(8,128)(2,1)} fusion(bf16[2304,96,32]{1,2,0:T(8,128)(2,1)} %get-tuple-element.309, s32[1024]{0:T(1024)S(1)} %pad_clamp_fusion.2), kind=kCustom, calls=%fused_computation.clone.clone.1 | custom fusion | bytes 6293504 | tf_op jit(solution)/shard_map/while/body/eval_jaxpr/jit(_take)/gather | solution.py:68
  610.1 5.8 copy.100
  621.4 9.6 %gather_fusion = bf16[512,96,32]{1,2,0:T(8,128)(2,1)} fusion(bf16[2304,96,32]{1,2,0:T(8,128)(2,1)} %get-tuple-element.309, s32[1024]{0:T(1024)S(1)} %pad_clamp_fusion.2), kind=kCustom, calls=%fused_computation.clone.clone.1 | custom fusion | bytes 6293504 | tf_op jit(solution)/shard_map/while/body/eval_jaxpr/jit(_take)/gather | solution.py:68
  631.0 5.8 copy.100
  642.2 9.6 %gather_fusion = bf16[512,96,32]{1,2,0:T(8,128)(2,1)} fusion(bf16[2304,96,32]{1,2,0:T(8,128)(2,1)} %get-tuple-element.309, s32[1024]{0:T(1024)S(1)} %pad_clamp_fusion.2), kind=kCustom, calls=%fused_computation.clone.clone.1 | custom fusion | bytes 6293504 | tf_op jit(solution)/shard_map/while/body/eval_jaxpr/jit(_take)/gather | solution.py:68
  651.8 5.8 copy.100
  663.1 9.6 %gather_fusion = bf16[512,96,32]{1,2,0:T(8,128)(2,1)} fusion(bf16[2304,96,32]{1,2,0:T(8,128)(2,1)} %get-tuple-element.309, s32[1024]{0:T(1024)S(1)} %pad_clamp_fusion.2), kind=kCustom, calls=%fused_computation.clone.clone.1 | custom fusion | bytes 6293504 | tf_op jit(solution)/shard_map/while/body/eval_jaxpr/jit(_take)/gather | solution.py:68
  672.7 5.8 copy.100
  684.0 9.6 %gather_fusion = bf16[512,96,32]{1,2,0:T(8,128)(2,1)} fusion(bf16[2304,96,32]{1,2,0:T(8,128)(2,1)} %get-tuple-element.309, s32[1024]{0:T(1024)S(1)} %pad_clamp_fusion.2), kind=kCustom, calls=%fused_computation.clone.clone.1 | custom fusion | bytes 6293504 | tf_op jit(solution)/shard_map/while/body/eval_jaxpr/jit(_take)/gather | solution.py:68
  693.6 5.8 copy.100
  704.8 9.6 %gather_fusion = bf16[512,96,32]{1,2,0:T(8,128)(2,1)} fusion(bf16[2304,96,32]{1,2,0:T(8,128)(2,1)} %get-tuple-element.309, s32[1024]{0:T(1024)S(1)} %pad_clamp_fusion.2), kind=kCustom, calls=%fused_computation.clone.clone.1 | custom fusion | bytes 6293504 | tf_op jit(solution)/shard_map/while/body/eval_jaxpr/jit(_take)/gather | solution.py:68
  714.4 5.8 copy.100
  725.9 41.7 %all-reduce.2.cloned.1.call-done = bf16[2,16,6144]{2,1,0:T(8,128)(2,1)} async-done(((bf16[2,16,6144]{2,1,0:T(8,128)(2,1)}), bf16[2,16,6144]{2,1,0:T(8,128)(2,1)}) %all-reduce.2.cloned.1.call-update) | async-done | bytes 393232 | tf_op jit(solution)/shard_map/psum | solution.py:118
  767.5 6.1 copy.55
  773.6 3.9 reshape.189
  777.5 5.1 all-to-all-start.2
  784.5 4.9 all-to-all-done.2
  791.4 8.8 %all-to-all-start.1 = ((bf16[32,2,16,1536]{3,2,1,0:T(8,128)(2,1)}), bf16[32,2,16,1536]{3,2,1,0:T(8,128)(2,1)S(1)}, u32[]{:S(2)}, u32[]{:S(2)}) async-start(bf16[32,2,16,1536]{3,2,1,0:T(8,128)(2,1)} %stack.21), calls=%async_computation.1 | async-start | bytes 6291456 | tf_op jit(solution)/shard_map/all_to_all | solution.py:128
  800.3 3.3 reshape.190
  803.6 8.0 copy.77
  812.0 36.2 %all-to-all-done.1 = bf16[32,2,16,1536]{3,2,1,0:T(8,128)(2,1)S(1)} async-done(((bf16[32,2,16,1536]{3,2,1,0:T(8,128)(2,1)}), bf16[32,2,16,1536]{3,2,1,0:T(8,128)(2,1)S(1)}, u32[]{:S(2)}, u32[]{:S(2)}) %all-to-all-start.1) | async-done | bytes 3145760 | tf_op jit(solution)/shard_map/all_to_all | solution.py:128
  (256 shorter events, 107.2 us)
Async XLA Ops:
  19.7 4.1 copy-start
  51.9 4.1 copy-start
  84.1 4.1 copy-start
  116.3 4.1 copy-start
  135.3 7.8 copy-start.2
  135.3 214.0 %all-to-all-start = ((bf16[16,24,96,192]{3,1,0,2:T(8,128)(2,1)}), bf16[16,24,96,192]{3,1,0,2:T(8,128)(2,1)}, u32[]{:S(2)}, u32[]{:S(2)}) async-start(bf16[16,24,96,192]{3,1,0,2:T(8,128)(2,1)} %bitcast.130), calls=%async_computation | async-start | bytes 37748736 | tf_op jit(solution)/shard_map/all_to_all | solution.py:114
  143.0 624.5 %all-reduce.2.cloned.1.call-start = ((), (), s32[]{:S(2)}) async-start(), calls=%async_computation.3 | async-start | bytes 786432 | tf_op jit(solution)/shard_map/psum | solution.py:118
  474.7 0.6 copy-start.3
  491.2 4.3 copy-start.4
  495.6 0.6 copy-start.3
  512.1 4.3 copy-start.4
  516.5 0.6 copy-start.3
  533.0 4.3 copy-start.4
  537.3 0.6 copy-start.3
  553.8 4.3 copy-start.4
  558.2 0.6 copy-start.3
  574.7 4.3 copy-start.4
  579.0 0.6 copy-start.3
  595.5 4.3 copy-start.4
  599.9 0.6 copy-start.3
  616.4 4.3 copy-start.4
  620.8 0.6 copy-start.3
  637.3 4.3 copy-start.4
  641.6 0.6 copy-start.3
  658.1 4.3 copy-start.4
  662.5 0.6 copy-start.3
  679.0 4.3 copy-start.4
  683.4 0.6 copy-start.3
  699.9 4.3 copy-start.4
  704.2 0.6 copy-start.3
  720.7 4.3 copy-start.4
  777.5 11.9 %all-to-all-start.2 = ((bf16[8,2,12288]{2,1,0:T(2,128)(2,1)}), bf16[8,2,12288]{2,1,0:T(2,128)(2,1)S(1)}, u32[]{:S(2)}, u32[]{:S(2)}) async-start(bf16[8,2,12288]{2,1,0:T(2,128)(2,1)} %reshape.189), calls=%async_computation.2 | async-start | bytes 786432 | tf_op jit(solution)/shard_map/all_to_all | solution.py:143
  791.4 56.7 %all-to-all-start.1 = ((bf16[32,2,16,1536]{3,2,1,0:T(8,128)(2,1)}), bf16[32,2,16,1536]{3,2,1,0:T(8,128)(2,1)S(1)}, u32[]{:S(2)}, u32[]{:S(2)}) async-start(bf16[32,2,16,1536]{3,2,1,0:T(8,128)(2,1)} %stack.21), calls=%async_computation.1 | async-start | bytes 6291456 | tf_op jit(solution)/shard_map/all_to_all | solution.py:128
  800.2 11.4 %copy-start.5 = (f32[32]{0:T(128)S(1)}, f32[32]{0:T(128)}, u32[]{:S(2)}) copy-start(f32[32]{0:T(128)} %param.12) | copy-start | bytes 388
  800.2 11.4 %copy-start.6 = (f32[16]{0:T(128)S(1)}, f32[16]{0:T(128)}, u32[]{:S(2)}) copy-start(f32[16]{0:T(128)} %param.11) | copy-start | bytes 196
  800.2 48.4 %all-gather.2.cloned.1.call-start = ((), (), s32[]{:S(2)}) async-start(), calls=%async_computation.4 | async-start | bytes 1966080 | tf_op jit(solution)/shard_map/all_gather | solution.py:145
  848.7 3.4 copy-start.1
Sparse Core Ops, SparseCore 0:
  726.0 41.4 all-reduce.1
  811.7 32.7 all-gather.1
